TPU v7x, 128 devices: a whole 4x4x4 slice. The times are simulated.
128 devices in a mesh: gx: 8 (over x_lo, y), gy: 16 (over z, x_hi, core).
Axes of the slice: x: 4 (x_hi: 2, x_lo: 2; x = x_hi * 2 + x_lo), y: 4, z: 4, core: 2. Of those that a mesh axis runs over, the one named last changes fastest.
Arguments:
- voxel_feats: bfloat16 [512, 64, 128], P(('gx', 'gy')), may hold values from -6 to 6
- w_first: bfloat16 [27, 128, 128], replicated, may hold values from -0.109375 to 0.109375
- w_second: bfloat16 [27, 128, 128], replicated, may hold values from -0.109375 to 0.109375
- norm_gain: float32 [2, 128], replicated, may hold values from 0.5 to 1.5
- norm_shift: float32 [2, 128], replicated, may hold values from -3 to 3
- grad_out: bfloat16 [512, 64, 128], P(('gx', 'gy')), may hold values from -6 to 6
- brick_count: int32 [128], P(('gx', 'gy')), may hold values from 1 to 4, as said below
- kernel_map: int32 [512, 27], P(('gx', 'gy')), may hold values from 0 to 12, as said below
- face_send: int32 [128, 4, 1], P(('gx', 'gy')), may hold values from 0 to 3, as said below
- corner_send: int32 [128, 4, 1], P(('gx', 'gy')), may hold values from 0 to 3, as said below
Outputs:
- out_feats: bfloat16 [512, 64, 128], P(('gx', 'gy'))
- grad_in: bfloat16 [512, 64, 128], P(('gx', 'gy'))
- weight_grads: float32 [2, 27, 128, 128], replicated
- norm_grads: float32 [4, 128], replicated
Inputs may be any that keep to these rules, and one draw needn't show every extreme that they name: `brick_count`: some tile is full in every draw. `kernel_map`: direction 13 names the brick itself; index 12 is the zero brick. `face_send`: list k names bricks of the tile below its brick_count, sent to its +x, -x, +y, -y neighbour for k = 0, 1, 2, 3. `corner_send`: list k names bricks of the tile below its brick_count, sent to its (+x, +y), (+x, -y), (-x, +y), (-x, -y) neighbour for k = 0, 1, 2, 3.
All inputs are finite; a program needn't handle non-finite values.
Results may differ from a plain program's by a relative error of at most 0.006.
Values may be sent and summed in bfloat16 or wider, within the bound.
No kernel may reach another device: no remote copies, remote signals or barrier semaphores. Data moves between devices by JAX's collectives and lax.ppermute only.
A program may use at most 128 MiB of HBM per device.

v0:
```python
import functools

import jax
import jax.numpy as jnp
import numpy as np
from jax import lax
from jax.experimental import pallas as pl
from jax.experimental.pallas import tpu as pltpu
from jax.sharding import Mesh
from jax.sharding import PartitionSpec as P

GX = ("gx_0", "gx_1")
GY = ("gy_0", "gy_1", "gy_2")
GX_GY = ("gx_0", "gx_1", "gy_0", "gy_1", "gy_2")
CORE = ("gy_2",)
X_LINE = "gx_1"
Y_LINE = "gy_2"
CHIPS = ("gx_0", "gx_1", "gy_0", "gy_1")
C = 128
NB = 4
ROWS = NB * 64
TAPS = 27
EXT = 13
EPSILON = 1e-05
F32 = jnp.float32
BF16 = jnp.bfloat16
COUNT, FACE, CORNER, VALID, CORE_AT = 108, 109, 113, 117, 125
NEIGHBOURS = ((-1, 0), (1, 0), (0, -1), (0, 1), (-1, -1), (-1, 1), (1, -1), (1, 1))
CHUNK = 56
HALF = TAPS * C // 2
VMEM_BYTES = 16 << 20


def row_of(k):
    return slice(k, k + 1)


VOXELS = row_of(0)
RECIP = (row_of(1), row_of(2))
NORM_ROWS = slice(4, 8)
GAIN = (row_of(4), row_of(5))
SHIFT = (row_of(6), row_of(7))
CROSS = (row_of(8), row_of(9))
TOTAL = (row_of(10), row_of(11))


def shift_matrix(flipped):
    def places(axis):
        at = lax.broadcasted_iota(jnp.int32, (144, 144), axis)
        major = (at >= 48).astype(jnp.int32) + (at >= 96).astype(jnp.int32)
        minor = (at >> 4) - 3 * major
        return major, minor, (at >> 2) & 3, at & 3

    b, c, q, r = places(1 if flipped else 0)
    ob, oc, qs, rs = places(0 if flipped else 1)
    hit = (4 * ob + qs == q + b + 3) & (4 * oc + rs == r + c + 3)
    return hit.astype(F32).astype(BF16)


def sources():
    return [(0, 0, 3), (1, 1, 0), (2, 1, 1), (3, 1, 2), (4, 1, 3), (5, 2, 0)]


def sigmoid(v):
    return 1.0 / (1.0 + jnp.exp(-v))


def slope(v):
    s = sigmoid(v)
    return s * (1.0 + v * (1.0 - s))


def occupied_rows(meta):
    brick = lax.broadcasted_iota(jnp.int32, (ROWS, C), 0) // 64
    return (brick < meta[COUNT]).astype(F32)


def shifted_planes(meta, ext, gathered, planes):
    shift = shift_matrix(False)
    for b in range(NB):
        for plane, oa, source in sources():
            for d in range(9):
                entry = meta[27 * b + 9 * oa + d]
                gathered[16 * d : 16 * d + 16, (6 * b + plane) * C : (6 * b + plane + 1) * C] = ext[
                    entry, 16 * source : 16 * source + 16, :
                ]
    for b in range(NB):
        at = slice(6 * b * C, 6 * (b + 1) * C)
        planes[:, at] = jnp.dot(shift, gathered[:, at], preferred_element_type=F32).astype(BF16)


def patches(planes, k):
    a, d = divmod(k, 9)
    tiles = [
        planes[16 * d : 16 * d + 16, (6 * b + p + a) * C : (6 * b + p + a + 1) * C]
        for b in range(NB)
        for p in range(4)
    ]
    return jnp.concatenate(tiles, axis=0)


def convolve(planes, weight):
    total = jnp.zeros((ROWS, C), F32)
    for k in range(0, TAPS, 2):
        taps = range(k, min(k + 2, TAPS))
        columns = jnp.concatenate([patches(planes, tap) for tap in taps], axis=1)
        total += jnp.dot(
            columns, weight[k * C : (k + len(taps)) * C, :], preferred_element_type=F32
        )
    return total


def convolve_back(meta, dz, weight, spread, moved, acc):
    shift_back = shift_matrix(True)
    for a in range(3):
        spread[a] = lax.dot_general(
            dz,
            weight[9 * a * C : 9 * (a + 1) * C, :],
            (((1,), (1,)), ((), ())),
            preferred_element_type=F32,
        )
    acc[...] = jnp.zeros_like(acc)
    for b in range(NB):
        for plane in range(6):
            taps = [a for a in range(3) if 0 <= plane - a < 4]
            for d in range(9):
                total = None
                for a in taps:
                    row = 64 * b + 16 * (plane - a)
                    piece = spread[a, row : row + 16, d * C : (d + 1) * C]
                    total = piece if total is None else total + piece
                moved[16 * d : 16 * d + 16, (6 * b + plane) * C : (6 * b + plane + 1) * C] = (
                    total.astype(BF16)
                )
    for b in range(NB):
        home = jnp.dot(
            shift_back, moved[:, 6 * b * C : 6 * (b + 1) * C], preferred_element_type=F32
        )
        for plane, oa, source in sources():
            for d in range(9):
                entry = meta[27 * b + 9 * oa + d]
                acc[entry, 16 * source : 16 * source + 16, :] += home[
                    16 * d : 16 * d + 16, plane * C : (plane + 1) * C
                ]


def write_sums(out, first, second):
    odd = lax.broadcasted_iota(jnp.int32, (8, C), 0) % 2
    both = jnp.where(odd == 0, jnp.broadcast_to(first, (8, C)), jnp.broadcast_to(second, (8, C)))
    out[...] = jnp.broadcast_to(both[None], (out.shape[0] // 8, 8, C)).reshape(out.shape)


def read_sums(got):
    total = jnp.sum(got[...].reshape(got.shape[0] // 8, 8, C), axis=0)
    odd = lax.broadcasted_iota(jnp.int32, (8, C), 0) % 2
    first = jnp.sum(jnp.where(odd == 0, total, 0.0), axis=0, keepdims=True)
    second = jnp.sum(jnp.where(odd == 1, total, 0.0), axis=0, keepdims=True)
    return first, second


def rows_sum(v):
    return jnp.sum(v, axis=0, keepdims=True)


def statistics(total, squares, voxels):
    center = total / voxels
    spread_sq = squares / voxels - center * center
    return center, lax.rsqrt(spread_sq + EPSILON)


def parity(axis):
    return 1 - lax.rem(lax.axis_index(axis), 2)


def from_next(near, far, even, k):
    return jnp.where(even == 1, near[k], far[k])


def from_previous(near, far, even, k):
    return jnp.where(even == 1, far[k], near[k])


def received_bricks(x_near, x_far, y_near, y_far):
    ex, ey = parity(X_LINE), parity(Y_LINE)
    return (
        from_previous(x_near, x_far, ex, 0), from_next(x_near, x_far, ex, 0),
        from_previous(y_near, y_far, ey, 0), from_next(y_near, y_far, ey, 0),
        from_previous(x_near, x_far, ex, 1), from_previous(x_near, x_far, ex, 2),
        from_next(x_near, x_far, ex, 1), from_next(x_near, x_far, ex, 2),
    )


def sends_of(face, corner, y_near, y_far, x_faces):
    even = parity(Y_LINE)

    def either(number, up, low):
        return jnp.where(even == number, up, low)

    up = (face(2), corner(0), corner(2))
    low = (face(3), corner(1), corner(3))
    pairs = [(face(0), x_faces.at[0]), (face(1), x_faces.at[1])]
    for k in range(3):
        pairs.append((either(1, up[k], low[k]), y_near.at[k]))
        pairs.append((either(0, up[k], low[k]), y_far.at[k]))
    return pairs


def select_sends(meta, field, y_near, y_far, x_faces):
    for entry, out in sends_of(
        lambda k: meta[FACE + k], lambda k: meta[CORNER + k], y_near, y_far, x_faces
    ):
        out[...] = field[entry]


def send_kernel(face_far, corner_far, field, y_near, y_far, x_faces, kept, face, corner, sems):
    copies = [
        pltpu.make_async_copy(field, kept, sems.at[0]),
        pltpu.make_async_copy(face_far, face, sems.at[1]),
        pltpu.make_async_copy(corner_far, corner, sems.at[2]),
    ]
    for copy in copies:
        copy.start()
    for copy in copies:
        copy.wait()
    for entry, out in sends_of(lambda k: face[k], lambda k: corner[k], y_near, y_far, x_faces):
        out[...] = kept[entry]


def fetch_one_kernel(far, out, sem):
    copy = pltpu.make_async_copy(far, out, sem)
    copy.start()
    copy.wait()


def fetch_two_kernel(far, out, sem):
    copy = pltpu.make_async_copy(far, out, sem)
    copy.start()
    copy.wait()


def join_kernel(faces, y_near, y_far, x_near, x_far, *, home):
    ex, ey = parity(X_LINE), parity(Y_LINE)
    before = [from_previous(y_near, y_far, ey, k) for k in (1, 2)]
    after = [from_next(y_near, y_far, ey, k) for k in (1, 2)]
    if home:
        low, up = ((faces[k], after[k], before[k]) for k in range(2))
    else:
        up, low = ((faces[k], before[k], after[k]) for k in range(2))
    for k in range(3):
        x_near[k] = jnp.where(ex == 1, up[k], low[k])
        x_far[k] = jnp.where(ex == 1, low[k], up[k])


def first_kernel(
    meta, voxel_feats, x_near, x_far, y_near, y_far, weight,
    z_out, ext, sums, y_near_out, y_far_out, x_faces, gathered, planes,
):
    ext[NB + 8] = jnp.zeros((64, C), BF16)
    for b in range(NB):
        keep = (meta[COUNT] > b).astype(F32)
        ext[b] = (voxel_feats[b].astype(F32) * keep).astype(BF16)
    for e, brick in enumerate(received_bricks(x_near, x_far, y_near, y_far)):
        keep = meta[VALID + e].astype(F32)
        ext[NB + e] = (brick.astype(F32) * keep).astype(BF16)
    shifted_planes(meta, ext, gathered, planes)
    z = convolve(planes, weight)
    z_out[...] = z.reshape(NB, 64, C)
    select_sends(meta, z_out, y_near_out, y_far_out, x_faces)
    masked = z * occupied_rows(meta)
    row = lax.broadcasted_iota(jnp.int32, (8, C), 0) % 4
    count = (64 * meta[COUNT]).astype(F32)
    part = jnp.where(
        row == 0, rows_sum(masked), jnp.where(row == 1, rows_sum(z * masked), count)
    )
    sums[...] = jnp.broadcast_to(part[None], (64, 8, C)).reshape(512, C)


def second_kernel(
    meta, got, z_one, x_near, x_far, y_near, y_far, norm, weight,
    z_out, ext, sums, xh_out, consts, gathered, planes,
):
    row = lax.broadcasted_iota(jnp.int32, (8, C), 0) % 4
    both = jnp.sum(got[...].reshape(64, 8, C), axis=0)
    total = rows_sum(jnp.where(row == 0, both, 0.0))
    squares = rows_sum(jnp.where(row == 1, both, 0.0))
    voxels = rows_sum(jnp.where(row == 2, both, 0.0))
    center, recip = statistics(total, squares, voxels)
    consts[...] = jnp.zeros_like(consts)
    consts[VOXELS] = voxels
    consts[RECIP[0]] = recip
    consts[NORM_ROWS] = norm[...]
    received = received_bricks(x_near, x_far, y_near, y_far)
    for e in range(EXT - 1):
        keep = meta[COUNT] > e if e < NB else meta[VALID + e - NB] > 0
        field = z_one[e] if e < NB else received[e - NB]
        xh = (field - center) * recip
        xh_out[e] = xh
        u = norm[0:1] * xh + norm[2:3]
        ext[e] = (u * sigmoid(u) * keep.astype(F32)).astype(BF16)
    ext[EXT - 1] = jnp.zeros((64, C), BF16)
    shifted_planes(meta, ext, gathered, planes)
    z = convolve(planes, weight)
    z_out[...] = z
    masked = z * occupied_rows(meta)
    write_sums(sums, rows_sum(masked), rows_sum(z * masked))


def third_kernel(
    meta, got, constants, z_two, voxel_feats, grad_out, out_feats, dv_out, xh_out, consts, sums
):
    total, squares = read_sums(got)
    center, recip = statistics(total, squares, constants[VOXELS])
    consts[...] = constants[...]
    consts[RECIP[1]] = recip
    occupied = occupied_rows(meta)
    xh = (z_two[...] - center) * recip
    xh_out[...] = xh
    feats = voxel_feats[...].astype(F32) * occupied
    pre = constants[GAIN[1]] * xh + constants[SHIFT[1]] + feats
    s = sigmoid(pre)
    out_feats[...] = (pre * s * occupied).astype(BF16)
    dv = grad_out[...].astype(F32) * occupied * (s * (1.0 + pre * (1.0 - s)))
    dv_out[...] = dv
    write_sums(sums, rows_sum(dv), rows_sum(dv * xh))


def norm_back(dv, xh, consts, number, total, cross, occupied):
    voxels = consts[VOXELS]
    scale = occupied * consts[GAIN[number]] * consts[RECIP[number]]
    return (scale * (dv - total / voxels - xh * cross / voxels)).astype(BF16)


def send_gradients(acc, own, y_near, y_far, x_faces):
    even = parity(Y_LINE)
    own[...] = acc[0:NB].reshape(ROWS, C)
    for k in range(3):
        y_near[k] = acc[NB + 2 + 2 * k + even].astype(BF16)
        y_far[k] = acc[NB + 3 + 2 * k - even].astype(BF16)
    x_faces[0] = acc[NB].astype(BF16)
    x_faces[1] = acc[NB + 1].astype(BF16)


def fourth_kernel(
    meta, got, dv, xh_two, constants, xh_one, weight,
    dz_out, own, y_near_out, y_far_out, x_faces, sums, consts, spread, moved, acc,
):
    total, cross = read_sums(got)
    consts[...] = constants[...]
    consts[CROSS[1]] = cross
    consts[TOTAL[1]] = total
    dz = norm_back(dv[...], xh_two[...], constants, 1, total, cross, occupied_rows(meta))
    dz_out[...] = dz
    convolve_back(meta, dz, weight, spread, moved, acc)
    send_gradients(acc, own, y_near_out, y_far_out, x_faces)
    first = jnp.zeros((64, C), F32)
    second = jnp.zeros((64, C), F32)
    for e in range(EXT - 1):
        keep = meta[COUNT] > e if e < NB else meta[VALID + e - NB] > 0
        xh = xh_one[e]
        du = acc[e] * slope(constants[GAIN[0]] * xh + constants[SHIFT[0]]) * keep.astype(F32)
        first += du
        second += du * xh
    write_sums(sums, rows_sum(first), rows_sum(second))


def add_returned(meta, field, x_near, x_far, y_near, y_far):
    back = received_bricks(x_near, x_far, y_near, y_far)
    for at, brick, neighbour in (
        (FACE, 1, 1), (FACE + 1, 0, 0), (FACE + 2, 3, 3), (FACE + 3, 2, 2),
        (CORNER, 6, 7), (CORNER + 1, 7, 6), (CORNER + 2, 4, 5), (CORNER + 3, 5, 4),
    ):
        field[meta[at]] += back[brick].astype(F32) * meta[VALID + neighbour].astype(F32)


def fifth_kernel(
    meta, got, own_in, x_near, x_far, y_near, y_far, xh_one, constants, dz_out, consts, field
):
    total, cross = read_sums(got)
    consts[...] = constants[...]
    consts[CROSS[0]] = cross
    consts[TOTAL[0]] = total
    field[...] = own_in[...].reshape(NB, 64, C)
    add_returned(meta, field, x_near, x_far, y_near, y_far)
    occupied = occupied_rows(meta)
    xh = xh_one[0:NB].reshape(ROWS, C)
    du = field[...].reshape(ROWS, C) * occupied * slope(
        constants[GAIN[0]] * xh + constants[SHIFT[0]]
    )
    dz_out[...] = norm_back(du, xh, constants, 0, total, cross, occupied)


def back_kernel(
    meta, dz, weight_far, own, y_near_out, y_far_out, x_faces, weight, sem, spread, moved, acc
):
    fetch = pltpu.make_async_copy(weight_far, weight, sem)
    fetch.start()
    fetch.wait()
    convolve_back(meta, dz[...], weight, spread, moved, acc)
    send_gradients(acc, own, y_near_out, y_far_out, x_faces)


def taps_kernel(meta, ext, dz, mine, other, gathered, planes, taps):
    shifted_planes(meta, ext, gathered, planes)
    for k in range(TAPS):
        taps[k * C : (k + 1) * C, :] = lax.dot_general(
            patches(planes, k),
            dz[...],
            (((0,), (0,)), ((), ())),
            preferred_element_type=F32,
        )
    here = meta[CORE_AT] == 0
    mine[30:32] = jnp.zeros((2, CHUNK, C), F32)
    other[30:32] = jnp.zeros((2, CHUNK, C), BF16)
    for c in range(31):
        full = min(CHUNK, HALF - CHUNK * c)
        at = CHUNK * c
        low = taps[at : at + full, :]
        high = taps[HALF + at : HALF + at + full, :]
        mine[c, 0:full, :] = jnp.where(here, low, high)
        other[c, 0:full, :] = jnp.where(here, high, low).astype(BF16)


def second_sum_kernel(mine, received, out):
    out[...] = (mine[...] + received[...].astype(F32)).astype(BF16)


def first_sum_kernel(mine, received, second, out):
    out[0:32] = (mine[...] + received[...].astype(F32)).astype(BF16)
    out[32:64] = second[...]


def total_kernel(consts, pieces, out):
    total = jnp.sum(pieces[...].astype(F32), axis=0) / jnp.sqrt(consts[VOXELS])
    out[...] = jnp.broadcast_to(total.astype(BF16)[None], (64, CHUNK, C))


def last_kernel(
    meta, own, x_near, x_far, y_near, y_far, dv, consts, grad_in, norm_grads, field
):
    field[...] = own[...].reshape(NB, 64, C)
    add_returned(meta, field, x_near, x_far, y_near, y_far)
    total = (dv[...] + field[...].reshape(ROWS, C)) * occupied_rows(meta)
    grad_in[...] = total.astype(BF16)
    root = jnp.sqrt(consts[VOXELS])
    for row, at in enumerate((CROSS[0], TOTAL[0], CROSS[1], TOTAL[1])):
        norm_grads[row : row + 1] = consts[at] / root


def widen_kernel(core, half, *refs, partner):
    out, wide, sems = refs[-3:]
    at = 1 - core[0] if partner else core[0]
    copies = []
    for conv in range(2):
        for piece in range(4):
            for c in range(8 * piece, min(8 * piece + 8, 31)):
                full = min(CHUNK, HALF - CHUNK * c)
                wide[conv, CHUNK * c : CHUNK * c + full, :] = half[32 * conv + c].astype(F32)[
                    0:full
                ]
            first = 8 * CHUNK * piece
            rows = pl.ds(first, min(8 * CHUNK, HALF - first))
            copies.append(
                pltpu.make_async_copy(
                    wide.at[conv, rows], out.at[conv, at, rows], sems.at[4 * conv + piece]
                )
            )
            copies[-1].start()
    for copy in copies:
        copy.wait()


def local(kernel, outs, ins, scratch=(), far=()):
    vmem = pl.BlockSpec(memory_space=pltpu.VMEM)
    smem = pl.BlockSpec(memory_space=pltpu.SMEM)
    hbm = pl.BlockSpec(memory_space=pltpu.HBM)
    specs = [hbm if n in far else smem if a.ndim == 1 else vmem for n, a in enumerate(ins)]
    ins = [
        pltpu.with_memory_space_constraint(a, pltpu.HBM) if n in far else a
        for n, a in enumerate(ins)
    ]
    return pl.pallas_call(
        kernel,
        out_shape=[jax.ShapeDtypeStruct(s, d) for s, d in outs],
        in_specs=specs,
        out_specs=[vmem] * len(outs),
        scratch_shapes=[pltpu.VMEM(*s) if isinstance(s, tuple) else s for s in scratch],
        compiler_params=pltpu.CompilerParams(vmem_limit_bytes=VMEM_BYTES),
    )(*ins)


def widen(core, half, partner, before):
    held = [] if before is None else [before]
    far = pl.BlockSpec(memory_space=pltpu.HBM)
    return pl.pallas_call(
        functools.partial(widen_kernel, partner=partner),
        out_shape=jax.ShapeDtypeStruct((2, 2, HALF, C), F32),
        in_specs=[pl.BlockSpec(memory_space=pltpu.SMEM), pl.BlockSpec(memory_space=pltpu.VMEM)]
        + [far] * len(held),
        out_specs=far,
        scratch_shapes=[pltpu.VMEM((2, HALF, C), F32), pltpu.SemaphoreType.DMA((8,))],
        input_output_aliases={2: 0} if held else {},
        compiler_params=pltpu.CompilerParams(vmem_limit_bytes=VMEM_BYTES),
        name="widen_kernel",
    )(core, half, *held)


def exchange(value, axes):
    return lax.all_to_all(value, axes, 0, 0, tiled=True)


def swap(value):
    return lax.ppermute(value, CORE, [(0, 1), (1, 0)])


def swaps(near, far, axes):
    length = lax.axis_size(axes)
    odd = [(k, (k + 1) % length) for k in range(1, length, 2)]
    far = lax.ppermute(far, axes, odd + [(b, a) for a, b in odd])
    near = lax.ppermute(near, axes, [(k, k ^ 1) for k in range(length)])
    return near, far


def two_hops(y_near, y_far, x_faces, home):
    y_near, y_far = swaps(y_near, y_far, GY)
    outs = [(y_near.shape, y_near.dtype)] * 2
    x_near, x_far = local(functools.partial(join_kernel, home=home), outs, [x_faces, y_near, y_far])
    x_near, x_far = swaps(x_near, x_far, GX)
    return x_near, x_far, y_near, y_far


def program(
    voxel_feats,
    w_first,
    w_second,
    norm_gain,
    norm_shift,
    grad_out,
    brick_count,
    kernel_map,
    face_send,
    corner_send,
):
    face = face_send.reshape(4)
    corner = corner_send.reshape(4)
    i = lax.axis_index(GX)
    j = lax.axis_index(GY)
    dx = np.array([d[0] for d in NEIGHBOURS], np.int32)
    dy = np.array([d[1] for d in NEIGHBOURS], np.int32)
    inside = (i + dx >= 0) & (i + dx < 8) & (j + dy >= 0) & (j + dy < 16)
    meta = jnp.concatenate(
        [
            kernel_map.reshape(-1),
            brick_count,
            face,
            corner,
            inside.astype(jnp.int32),
            lax.axis_index(CORE).reshape(1),
        ]
    )
    norm = jnp.concatenate([norm_gain, norm_shift], axis=0)
    flat_one = w_first.reshape(TAPS * C, C)
    flat_two = w_second.reshape(TAPS * C, C)
    brick = (64, C)
    three, two = (3,) + brick, (2,) + brick
    rows = (ROWS, C)
    sums = ((2 * 128, C), F32)
    ext = ((EXT,) + brick, BF16)
    list_xh = ((EXT - 1,) + brick, F32)
    table = ((16, C), F32)
    sem = pltpu.SemaphoreType.DMA
    weight = ((TAPS * C, C), BF16)
    gathered = ((144, 6 * NB * C), BF16)
    forward = [gathered, gathered]

    *sends, kept = local(
        send_kernel,
        [(three, BF16), (three, BF16), (two, BF16), ((NB,) + brick, BF16)],
        [face, corner, voxel_feats],
        [pltpu.SMEM((4,), jnp.int32), pltpu.SMEM((4,), jnp.int32), sem((3,))],
        far=(0, 1, 2),
    )
    (near_one,) = local(fetch_one_kernel, [weight], [flat_one], [sem(())], far=(0,))
    (near_two,) = local(fetch_two_kernel, [weight], [flat_two], [sem(())], far=(0,))
    received = two_hops(*sends, False)
    z_one, ext_one, part, *sends = local(
        first_kernel,
        [((NB,) + brick, F32), ext, ((512, C), F32), (three, F32), (three, F32), (two, F32)],
        [meta, kept, *received, near_one],
        forward,
    )
    received = two_hops(*sends, False)
    part = exchange(part, GX_GY)
    z_two, ext_two, part, xh_one, consts = local(
        second_kernel,
        [(rows, F32), ext, sums, list_xh, table],
        [meta, part, z_one, *received, norm, near_two],
        forward,
    )
    part = exchange(part, GX_GY)
    out_feats, dv, xh_two, consts, part = local(
        third_kernel,
        [(rows, BF16), (rows, F32), (rows, F32), table, sums],
        [meta, part, consts, z_two, voxel_feats.reshape(rows), grad_out.reshape(rows)],
    )
    part = exchange(part, GX_GY)
    back = [((3, ROWS, 9 * C), F32), gathered, ((EXT,) + brick, F32)]
    dz_two, own, y_near, y_far, x_faces, part, consts = local(
        fourth_kernel,
        [(rows, BF16), (rows, F32), (three, BF16), (three, BF16), (two, BF16), sums, table],
        [meta, part, dv, xh_two, consts, xh_one, near_two],
        back,
    )
    returned = two_hops(y_near, y_far, x_faces, True)
    chunks = (32, CHUNK, C)
    halves = [(chunks, F32), (chunks, BF16)]
    products = [gathered, gathered, ((TAPS * C, C), F32)]
    mine, other = local(taps_kernel, halves, [meta, ext_two, dz_two], products)
    (second,) = local(second_sum_kernel, [(chunks, BF16)], [mine, swap(other)])
    part = exchange(part, GX_GY)
    dz_one, consts = local(
        fifth_kernel,
        [(rows, BF16), table],
        [meta, part, own, *returned, xh_one, consts],
        [((NB,) + brick, F32)],
    )
    own, y_near, y_far, x_faces = local(
        back_kernel,
        [(rows, F32), (three, BF16), (three, BF16), (two, BF16)],
        [meta, dz_one, flat_one],
        [weight, sem(())] + back,
        far=(2,),
    )
    returned = two_hops(y_near, y_far, x_faces, True)
    mine, other = local(taps_kernel, halves, [meta, ext_one, dz_one], products)
    grad_in, norm_grads = local(
        last_kernel,
        [(rows, BF16), ((4, C), F32)],
        [meta, own, *returned, dv, consts],
        [((NB,) + brick, F32)],
    )
    both = ((64, CHUNK, C), BF16)
    (part,) = local(first_sum_kernel, [both], [mine, swap(other), second])
    part = exchange(part, CHIPS)
    (whole,) = local(total_kernel, [both], [consts, part])
    whole = exchange(whole, CHIPS)
    partner = swap(whole)
    core = lax.axis_index(CORE).reshape(1)
    weight_grads = widen(core, whole, False, None)
    weight_grads = widen(core, partner, True, weight_grads).reshape(2, TAPS, C, C)
    return (
        out_feats.reshape(NB, 64, C),
        grad_in.reshape(NB, 64, C),
        weight_grads,
        norm_grads,
    )


def solution(mesh):
    split = Mesh(mesh.devices.reshape(2, 4, 4, 2, 2), GX_GY)
    in_specs = (
        P(GX_GY, None, None),
        P(),
        P(),
        P(),
        P(),
        P(GX_GY, None, None),
        P(GX_GY),
        P(GX_GY, None),
        P(GX_GY, None, None),
        P(GX_GY, None, None),
    )
    out_specs = (P(GX_GY, None, None), P(GX_GY, None, None), P(), P())
    return jax.shard_map(program, mesh=split, in_specs=in_specs, out_specs=out_specs, check_vma=False)
```

profile of v0, /device:TPU:0, one launch (start us, length us, event | category | flops | bytes accessed | tf_op | source)
XLA Modules:
  0.0 174.9 jit_solution(5526157144644760480)
XLA Ops:
  1.7 6.7 %collective-permute-start.1 = (bf16[3,64,128]{2,1,0:T(8,128)(2,1)S(1)}, bf16[3,64,128]{2,1,0:T(8,128)(2,1)S(1)}, u32[]{:S(2)}, u32[]{:S(2)}) collective-permute-start(bf16[3,64,128]{2,1,0:T(8,128)(2,1)S(1)} %get-tuple-element.54), channel_id=1, source_target_pairs={{1,2},{3,4},{5,6},{7,8},{9,10},{11,12},{13,14},{15,0},{2,1},{4,3},... | collective-permute-start | bytes 147464 | tf_op jit(solution)/shard_map/ppermute | solution.py:518
  8.4 1.8 %collective-permute-done.1.y_far = bf16[3,64,128]{2,1,0:T(8,128)(2,1)S(1)} collective-permute-done((bf16[3,64,128]{2,1,0:T(8,128)(2,1)S(1)}, bf16[3,64,128]{2,1,0:T(8,128)(2,1)S(1)}, u32[]{:S(2)}, u32[]{:S(2)}) %collective-permute-start.1) | collective-permute-done | bytes 49184 | tf_op jit(solution)/shard_map/ppermute | solution.py:518
  11.8 2.2 %collective-permute-start.3 = (bf16[3,64,128]{2,1,0:T(8,128)(2,1)S(1)}, bf16[3,64,128]{2,1,0:T(8,128)(2,1)S(1)}, u32[]{:S(2)}, u32[]{:S(2)}) collective-permute-start(bf16[3,64,128]{2,1,0:T(8,128)(2,1)S(1)} %get-tuple-element.56), channel_id=1, source_target_pairs={{16,32},{48,64},{80,96},{112,0},{32,16},{64,48},{96,80},{0,112},{1... | collective-permute-start | bytes 147464 | tf_op jit(solution)/shard_map/ppermute | solution.py:518
  18.1 2.3 %shard_map.150 = (f32[4,64,128]{2,1,0:T(8,128)S(1)}, bf16[13,64,128]{2,1,0:T(8,128)(2,1)S(1)}, f32[512,128]{1,0:T(8,128)}, f32[3,64,128]{2,1,0:T(8,128)S(1)}, f3...) custom-call(s32[126]{0:T(128)S(1)} %concatenate.6.meta, bf16[4,64,128]{2,1,0:T(8,128)(2,1)S(1)} %get-tuple-element.51.voxel_feats, ...), custom_call_target="tpu_custom_call" | custom-call | tf_op jit(solution)/shard_map/pallas_call | solution.py:481
  20.5 7.8 %all-to-all-start = ((f32[128,4,128]{2,1,0:T(4,128)}), f32[128,4,128]{2,1,0:T(4,128)S(1)}, u32[]{:S(2)}, u32[]{:S(2)}) async-start(f32[128,4,128]{2,1,0:T(4,128)} %bitcast.4), calls=%async_computation | async-start | bytes 524288 | tf_op jit(solution)/shard_map/all_to_all | solution.py:508
  28.4 5.4 %collective-permute-start.5 = (f32[3,64,128]{2,1,0:T(8,128)S(1)}, f32[3,64,128]{2,1,0:T(8,128)S(1)}, u32[]{:S(2)}, u32[]{:S(2)}) collective-permute-start(f32[3,64,128]{2,1,0:T(8,128)S(1)} %get-tuple-element.61), channel_id=1, source_target_pairs={{1,2},{3,4},{5,6},{7,8},{9,10},{11,12},{13,14},{15,0},{2,1},{4,3},... | collective-permute-start | bytes 294920 | tf_op jit(solution)/shard_map/ppermute | solution.py:518
  34.9 3.3 %collective-permute-done.5.y_far = f32[3,64,128]{2,1,0:T(8,128)S(1)} collective-permute-done((f32[3,64,128]{2,1,0:T(8,128)S(1)}, f32[3,64,128]{2,1,0:T(8,128)S(1)}, u32[]{:S(2)}, u32[]{:S(2)}) %collective-permute-start.5) | collective-permute-done | bytes 98336 | tf_op jit(solution)/shard_map/ppermute | solution.py:518
  39.9 2.2 %collective-permute-start.7 = (f32[3,64,128]{2,1,0:T(8,128)S(1)}, f32[3,64,128]{2,1,0:T(8,128)S(1)}, u32[]{:S(2)}, u32[]{:S(2)}) collective-permute-start(f32[3,64,128]{2,1,0:T(8,128)S(1)} %get-tuple-element.63), channel_id=1, source_target_pairs={{16,32},{48,64},{80,96},{112,0},{32,16},{64,48},{96,80},{0,112},{1... | collective-permute-start | bytes 294920 | tf_op jit(solution)/shard_map/ppermute | solution.py:518
  43.0 3.6 %collective-permute-done.7.x_far = f32[3,64,128]{2,1,0:T(8,128)S(1)} collective-permute-done((f32[3,64,128]{2,1,0:T(8,128)S(1)}, f32[3,64,128]{2,1,0:T(8,128)S(1)}, u32[]{:S(2)}, u32[]{:S(2)}) %collective-permute-start.7) | collective-permute-done | bytes 98336 | tf_op jit(solution)/shard_map/ppermute | solution.py:518
  46.6 1.8 %shard_map.153 = (f32[256,128]{1,0:T(8,128)S(1)}, bf16[13,64,128]{2,1,0:T(8,128)(2,1)S(1)}, f32[256,128]{1,0:T(8,128)S(1)}, f32[12,64,128]{2,1,0:T(8,128)S(1)}, f32[16,128]{1,0:T(8,128)S(1)}) custom-call(s32[126]{0:T(128)S(1)} %concatenate.6.meta, f32[512,128]{1,0:T(8,128)S(1)} %bitcast.18, f32[4,64,128]{2,1,0:T(8,128)S(1)} %get-tuple-element.58.z_one, ...), custom_call_target="tpu_custom_call" | custom-call | tf_op jit(solution)/shard_map/pallas_call | solution.py:481
  48.4 15.5 %all_to_all.54 = f32[128,2,128]{2,1,0:T(2,128)S(1)} all-to-all(f32[128,2,128]{2,1,0:T(2,128)S(1)} %bitcast.23), channel_id=1, replica_groups=mesh['gx_0'=2,'gx_1'=4,'gy_0'=4,'gy_1'=2,'gy_2'=2] {'gx_0','gx_1','gy_0'..., dimensions={0} | all-to-all | bytes 262144 | tf_op jit(solution)/shard_map/all_to_all | solution.py:508
  65.2 14.2 %all_to_all.55 = f32[128,2,128]{2,1,0:T(2,128)S(1)} all-to-all(f32[128,2,128]{2,1,0:T(2,128)S(1)} %bitcast.24), channel_id=1, replica_groups=mesh['gx_0'=2,'gx_1'=4,'gy_0'=4,'gy_1'=2,'gy_2'=2] {'gx_0','gx_1','gy_0'..., dimensions={0} | all-to-all | bytes 262144 | tf_op jit(solution)/shard_map/all_to_all | solution.py:508
  79.3 2.9 %shard_map.155 = (bf16[256,128]{1,0:T(8,128)(2,1)S(1)}, f32[256,128]{1,0:T(8,128)S(1)}, bf16[3,64,128]{2,1,0:T(8,128)(2,1)S(1)}, bf16[3,64,128]{2,1,0:T(8,128)(2...) custom-call(s32[126]{0:T(128)S(1)} %concatenate.6.meta, ...), custom_call_target="tpu_custom_call" | custom-call | tf_op jit(solution)/shard_map/pallas_call | solution.py:481
  82.2 4.9 %all-to-all-start.3 = ((f32[128,2,128]{2,1,0:T(2,128)}), f32[128,2,128]{2,1,0:T(2,128)S(1)}, u32[]{:S(2)}, u32[]{:S(2)}) async-start(f32[128,2,128]{2,1,0:T(2,128)} %bitcast.14), calls=%async_computation.3 | async-start | bytes 262144 | tf_op jit(solution)/shard_map/all_to_all | solution.py:508
  87.2 5.4 %collective-permute-start.9 = (bf16[3,64,128]{2,1,0:T(8,128)(2,1)S(1)}, bf16[3,64,128]{2,1,0:T(8,128)(2,1)S(1)}, u32[]{:S(2)}, u32[]{:S(2)}) collective-permute-start(bf16[3,64,128]{2,1,0:T(8,128)(2,1)S(1)} %get-tuple-element.77), channel_id=1, source_target_pairs={{1,2},{3,4},{5,6},{7,8},{9,10},{11,12},{13,14},{15,0},{2,1},{4,3},... | collective-permute-start | bytes 147464 | tf_op jit(solution)/shard_map/ppermute | solution.py:518
  92.6 2.2 %collective-permute-done.9.y_far = bf16[3,64,128]{2,1,0:T(8,128)(2,1)S(1)} collective-permute-done((bf16[3,64,128]{2,1,0:T(8,128)(2,1)S(1)}, bf16[3,64,128]{2,1,0:T(8,128)(2,1)S(1)}, u32[]{:S(2)}, u32[]{:S(2)}) %collective-permute-start.9) | collective-permute-done | bytes 49184 | tf_op jit(solution)/shard_map/ppermute | solution.py:518
  96.4 2.1 %collective-permute-start.11 = (bf16[3,64,128]{2,1,0:T(8,128)(2,1)S(1)}, bf16[3,64,128]{2,1,0:T(8,128)(2,1)S(1)}, u32[]{:S(2)}, u32[]{:S(2)}) collective-permute-start(bf16[3,64,128]{2,1,0:T(8,128)(2,1)S(1)} %get-tuple-element.79), channel_id=1, source_target_pairs={{16,32},{48,64},{80,96},{112,0},{32,16},{64,48},{96,80},{0,112},{1... | collective-permute-start | bytes 147464 | tf_op jit(solution)/shard_map/ppermute | solution.py:518
  100.4 2.2 %collective-permute-done.11.x_far = bf16[3,64,128]{2,1,0:T(8,128)(2,1)S(1)} collective-permute-done((bf16[3,64,128]{2,1,0:T(8,128)(2,1)S(1)}, bf16[3,64,128]{2,1,0:T(8,128)(2,1)S(1)}, u32[]{:S(2)}, u32[]{:S(2)}) %collective-permute-start.11) | collective-permute-done | bytes 49184 | tf_op jit(solution)/shard_map/ppermute | solution.py:518
  107.0 25.0 %all_to_all.56.pieces = bf16[64,56,128]{2,1,0:T(8,128)(2,1)S(1)} all-to-all(bf16[64,56,128]{2,1,0:T(8,128)(2,1)S(1)} %shard_map.164), channel_id=1, replica_groups=mesh['gx_0'=2,'gx_1'=4,'gy_0'=4,'gy_1'=2,'gy_2'=2] {'gx_0','gx_1','gy_0'..., dimensions={0} | all-to-all | bytes 1835008 | tf_op jit(solution)/shard_map/all_to_all | solution.py:508
  132.1 20.9 %all_to_all.57.half = bf16[64,56,128]{2,1,0:T(8,128)(2,1)S(1)} all-to-all(bf16[64,56,128]{2,1,0:T(8,128)(2,1)S(1)} %shard_map.165), channel_id=1, replica_groups=mesh['gx_0'=2,'gx_1'=4,'gy_0'=4,'gy_1'=2,'gy_2'=2] {'gx_0','gx_1','gy_0'..., dimensions={0} | all-to-all | bytes 1835008 | tf_op jit(solution)/shard_map/all_to_all | solution.py:508
  153.1 3.2 %shard_map.158 = (f32[256,128]{1,0:T(8,128)S(1)}, bf16[3,64,128]{2,1,0:T(8,128)(2,1)S(1)}, bf16[3,64,128]{2,1,0:T(8,128)(2,1)S(1)}, bf16[2,64,128]{2,1,0:T(8,128)(2,1)S(1)}) custom-call(s32[126]{0:T(128)S(1)} %concatenate.6.meta, bf16[256,128]{1,0:T(8,128)(2,1)S(1)} %get-tuple-element.81.dz, bf16[3456,128]{1,0:T(8,128)(2,1)} %bitcast.28), custom_call_target="tpu_custom_call" | custom-call | tf_op jit(solution)/shard_map/pallas_call | solution.py:481
  158.0 5.9 %collective-permute-done.13.y_far = bf16[3,64,128]{2,1,0:T(8,128)(2,1)S(1)} collective-permute-done((bf16[3,64,128]{2,1,0:T(8,128)(2,1)S(1)}, bf16[3,64,128]{2,1,0:T(8,128)(2,1)S(1)}, u32[]{:S(2)}, u32[]{:S(2)}) %collective-permute-start.13) | collective-permute-done | bytes 49184 | tf_op jit(solution)/shard_map/ppermute | solution.py:518
  165.4 2.7 %collective-permute-done.14.x_near = bf16[3,64,128]{2,1,0:T(8,128)(2,1)S(1)} collective-permute-done((bf16[3,64,128]{2,1,0:T(8,128)(2,1)S(1)}, bf16[3,64,128]{2,1,0:T(8,128)(2,1)S(1)}, u32[]{:S(2)}, u32[]{:S(2)}) %collective-permute-start.14) | collective-permute-done | bytes 49184 | tf_op jit(solution)/shard_map/ppermute | solution.py:519
  168.1 2.7 %collective-permute-done.15.x_far = bf16[3,64,128]{2,1,0:T(8,128)(2,1)S(1)} collective-permute-done((bf16[3,64,128]{2,1,0:T(8,128)(2,1)S(1)}, bf16[3,64,128]{2,1,0:T(8,128)(2,1)S(1)}, u32[]{:S(2)}, u32[]{:S(2)}) %collective-permute-start.15) | collective-permute-done | bytes 49184 | tf_op jit(solution)/shard_map/ppermute | solution.py:518
  (55 shorter events, 26.4 us)
Async XLA Ops:
  0.6 41.4 %copy-start.2 = (f32[2,128]{1,0:T(2,128)S(1)}, f32[2,128]{1,0:T(2,128)}, u32[]{:S(2)}) copy-start(f32[2,128]{1,0:T(2,128)} %param.16) | copy-start | bytes 3076
  1.6 6.8 %collective-permute-start = (bf16[3,64,128]{2,1,0:T(8,128)(2,1)S(1)}, bf16[3,64,128]{2,1,0:T(8,128)(2,1)S(1)}, u32[]{:S(2)}, u32[]{:S(2)}) collective-permute-start(bf16[3,64,128]{2,1,0:T(8,128)(2,1)S(1)} %get-tuple-element.53), channel_id=1, source_target_pairs={{0,1},{1,0},{2,3},{3,2},{4,5},{5,4},{6,7},{7,6},{8,9},{9,8},{10,11... | collective-permute-start | bytes 147464 | tf_op jit(solution)/shard_map/ppermute | solution.py:519
  1.7 8.5 %collective-permute-start.1 = (bf16[3,64,128]{2,1,0:T(8,128)(2,1)S(1)}, bf16[3,64,128]{2,1,0:T(8,128)(2,1)S(1)}, u32[]{:S(2)}, u32[]{:S(2)}) collective-permute-start(bf16[3,64,128]{2,1,0:T(8,128)(2,1)S(1)} %get-tuple-element.54), channel_id=1, source_target_pairs={{1,2},{3,4},{5,6},{7,8},{9,10},{11,12},{13,14},{15,0},{2,1},{4,3},... | collective-permute-start | bytes 147464 | tf_op jit(solution)/shard_map/ppermute | solution.py:518
  10.2 7.9 %collective-permute-start.2 = (bf16[3,64,128]{2,1,0:T(8,128)(2,1)S(1)}, bf16[3,64,128]{2,1,0:T(8,128)(2,1)S(1)}, u32[]{:S(2)}, u32[]{:S(2)}) collective-permute-start(bf16[3,64,128]{2,1,0:T(8,128)(2,1)S(1)} %get-tuple-element.55), channel_id=1, source_target_pairs={{0,16},{16,0},{32,48},{48,32},{64,80},{80,64},{96,112},{112,96},{1... | collective-permute-start | bytes 147464 | tf_op jit(solution)/shard_map/ppermute | solution.py:519
  11.8 6.3 %collective-permute-start.3 = (bf16[3,64,128]{2,1,0:T(8,128)(2,1)S(1)}, bf16[3,64,128]{2,1,0:T(8,128)(2,1)S(1)}, u32[]{:S(2)}, u32[]{:S(2)}) collective-permute-start(bf16[3,64,128]{2,1,0:T(8,128)(2,1)S(1)} %get-tuple-element.56), channel_id=1, source_target_pairs={{16,32},{48,64},{80,96},{112,0},{32,16},{64,48},{96,80},{0,112},{1... | collective-permute-start | bytes 147464 | tf_op jit(solution)/shard_map/ppermute | solution.py:518
  16.1 47.7 %copy-start = (bf16[4,64,128]{2,1,0:T(8,128)(2,1)S(1)}, bf16[4,64,128]{2,1,0:T(8,128)(2,1)}, u32[]{:S(2)}) copy-start(bf16[4,64,128]{2,1,0:T(8,128)(2,1)} %field.1) | copy-start | bytes 196612
  16.1 47.7 %copy-start.1 = (bf16[4,64,128]{2,1,0:T(8,128)(2,1)S(1)}, bf16[4,64,128]{2,1,0:T(8,128)(2,1)}, u32[]{:S(2)}) copy-start(bf16[4,64,128]{2,1,0:T(8,128)(2,1)} %param.17) | copy-start | bytes 196612
  20.5 26.1 %all-to-all-start = ((f32[128,4,128]{2,1,0:T(4,128)}), f32[128,4,128]{2,1,0:T(4,128)S(1)}, u32[]{:S(2)}, u32[]{:S(2)}) async-start(f32[128,4,128]{2,1,0:T(4,128)} %bitcast.4), calls=%async_computation | async-start | bytes 524288 | tf_op jit(solution)/shard_map/all_to_all | solution.py:508
  28.3 6.6 %collective-permute-start.4 = (f32[3,64,128]{2,1,0:T(8,128)S(1)}, f32[3,64,128]{2,1,0:T(8,128)S(1)}, u32[]{:S(2)}, u32[]{:S(2)}) collective-permute-start(f32[3,64,128]{2,1,0:T(8,128)S(1)} %get-tuple-element.60), channel_id=1, source_target_pairs={{0,1},{1,0},{2,3},{3,2},{4,5},{5,4},{6,7},{7,6},{8,9},{9,8},{10,11... | collective-permute-start | bytes 294920 | tf_op jit(solution)/shard_map/ppermute | solution.py:519
  28.4 9.9 %collective-permute-start.5 = (f32[3,64,128]{2,1,0:T(8,128)S(1)}, f32[3,64,128]{2,1,0:T(8,128)S(1)}, u32[]{:S(2)}, u32[]{:S(2)}) collective-permute-start(f32[3,64,128]{2,1,0:T(8,128)S(1)} %get-tuple-element.61), channel_id=1, source_target_pairs={{1,2},{3,4},{5,6},{7,8},{9,10},{11,12},{13,14},{15,0},{2,1},{4,3},... | collective-permute-start | bytes 294920 | tf_op jit(solution)/shard_map/ppermute | solution.py:518
  38.3 4.7 %collective-permute-start.6 = (f32[3,64,128]{2,1,0:T(8,128)S(1)}, f32[3,64,128]{2,1,0:T(8,128)S(1)}, u32[]{:S(2)}, u32[]{:S(2)}) collective-permute-start(f32[3,64,128]{2,1,0:T(8,128)S(1)} %get-tuple-element.62), channel_id=1, source_target_pairs={{0,16},{16,0},{32,48},{48,32},{64,80},{80,64},{96,112},{112,96},{1... | collective-permute-start | bytes 294920 | tf_op jit(solution)/shard_map/ppermute | solution.py:519
  39.9 6.7 %collective-permute-start.7 = (f32[3,64,128]{2,1,0:T(8,128)S(1)}, f32[3,64,128]{2,1,0:T(8,128)S(1)}, u32[]{:S(2)}, u32[]{:S(2)}) collective-permute-start(f32[3,64,128]{2,1,0:T(8,128)S(1)} %get-tuple-element.63), channel_id=1, source_target_pairs={{16,32},{48,64},{80,96},{112,0},{32,16},{64,48},{96,80},{0,112},{1... | collective-permute-start | bytes 294920 | tf_op jit(solution)/shard_map/ppermute | solution.py:518
  82.2 20.4 %all-to-all-start.3 = ((f32[128,2,128]{2,1,0:T(2,128)}), f32[128,2,128]{2,1,0:T(2,128)S(1)}, u32[]{:S(2)}, u32[]{:S(2)}) async-start(f32[128,2,128]{2,1,0:T(2,128)} %bitcast.14), calls=%async_computation.3 | async-start | bytes 262144 | tf_op jit(solution)/shard_map/all_to_all | solution.py:508
  87.1 5.5 %collective-permute-start.8 = (bf16[3,64,128]{2,1,0:T(8,128)(2,1)S(1)}, bf16[3,64,128]{2,1,0:T(8,128)(2,1)S(1)}, u32[]{:S(2)}, u32[]{:S(2)}) collective-permute-start(bf16[3,64,128]{2,1,0:T(8,128)(2,1)S(1)} %get-tuple-element.76), channel_id=1, source_target_pairs={{0,1},{1,0},{2,3},{3,2},{4,5},{5,4},{6,7},{7,6},{8,9},{9,8},{10,11... | collective-permute-start | bytes 147464 | tf_op jit(solution)/shard_map/ppermute | solution.py:519
  87.2 7.6 %collective-permute-start.9 = (bf16[3,64,128]{2,1,0:T(8,128)(2,1)S(1)}, bf16[3,64,128]{2,1,0:T(8,128)(2,1)S(1)}, u32[]{:S(2)}, u32[]{:S(2)}) collective-permute-start(bf16[3,64,128]{2,1,0:T(8,128)(2,1)S(1)} %get-tuple-element.77), channel_id=1, source_target_pairs={{1,2},{3,4},{5,6},{7,8},{9,10},{11,12},{13,14},{15,0},{2,1},{4,3},... | collective-permute-start | bytes 147464 | tf_op jit(solution)/shard_map/ppermute | solution.py:518
  94.8 5.6 %collective-permute-start.10 = (bf16[3,64,128]{2,1,0:T(8,128)(2,1)S(1)}, bf16[3,64,128]{2,1,0:T(8,128)(2,1)S(1)}, u32[]{:S(2)}, u32[]{:S(2)}) collective-permute-start(bf16[3,64,128]{2,1,0:T(8,128)(2,1)S(1)} %get-tuple-element.78), channel_id=1, source_target_pairs={{0,16},{16,0},{32,48},{48,32},{64,80},{80,64},{96,112},{112,96},{1... | collective-permute-start | bytes 147464 | tf_op jit(solution)/shard_map/ppermute | solution.py:519
  96.4 6.2 %collective-permute-start.11 = (bf16[3,64,128]{2,1,0:T(8,128)(2,1)S(1)}, bf16[3,64,128]{2,1,0:T(8,128)(2,1)S(1)}, u32[]{:S(2)}, u32[]{:S(2)}) collective-permute-start(bf16[3,64,128]{2,1,0:T(8,128)(2,1)S(1)} %get-tuple-element.79), channel_id=1, source_target_pairs={{16,32},{48,64},{80,96},{112,0},{32,16},{64,48},{96,80},{0,112},{1... | collective-permute-start | bytes 147464 | tf_op jit(solution)/shard_map/ppermute | solution.py:518
  100.1 4.9 %collective-permute-start.17 = (bf16[32,56,128]{2,1,0:T(8,128)(2,1)S(1)}, bf16[32,56,128]{2,1,0:T(8,128)(2,1)S(1)}, u32[]{:S(2)}, u32[]{:S(2)}) collective-permute-start(bf16[32,56,128]{2,1,0:T(8,128)(2,1)S(1)} %get-tuple-element.96), channel_id=1, source_target_pairs={{0,1},{1,0},{2,3},{3,2},{4,5},{5,4},{6,7},{7,6},{8,9},{9,8},{10,11... | collective-permute-start | bytes 1376264 | tf_op jit(solution)/shard_map/ppermute | solution.py:512
  105.0 1.9 %collective-permute-start.16 = (bf16[32,56,128]{2,1,0:T(8,128)(2,1)S(1)}, bf16[32,56,128]{2,1,0:T(8,128)(2,1)S(1)}, u32[]{:S(2)}, u32[]{:S(2)}) collective-permute-start(bf16[32,56,128]{2,1,0:T(8,128)(2,1)S(1)} %get-tuple-element.92), channel_id=1, source_target_pairs={{0,1},{1,0},{2,3},{3,2},{4,5},{5,4},{6,7},{7,6},{8,9},{9,8},{10,11... | collective-permute-start | bytes 1376264 | tf_op jit(solution)/shard_map/ppermute | solution.py:512
  153.1 20.3 %collective-permute-start.18 = (bf16[64,56,128]{2,1,0:T(8,128)(2,1)S(1)}, bf16[64,56,128]{2,1,0:T(8,128)(2,1)S(1)}, u32[]{:S(2)}, u32[]{:S(2)}) collective-permute-start(bf16[64,56,128]{2,1,0:T(8,128)(2,1)S(1)} %all_to_all.57.half), channel_id=1, source_target_pairs={{0,1},{1,0},{2,3},{3,2},{4,5},{5,4},{6,7},{7,6},{8,9},{9,8},{10,11... | collective-permute-start | bytes 2752520 | tf_op jit(solution)/shard_map/ppermute | solution.py:512
  156.3 1.8 %collective-permute-start.12 = (bf16[3,64,128]{2,1,0:T(8,128)(2,1)S(1)}, bf16[3,64,128]{2,1,0:T(8,128)(2,1)S(1)}, u32[]{:S(2)}, u32[]{:S(2)}) collective-permute-start(bf16[3,64,128]{2,1,0:T(8,128)(2,1)S(1)} %get-tuple-element.84), channel_id=1, source_target_pairs={{0,1},{1,0},{2,3},{3,2},{4,5},{5,4},{6,7},{7,6},{8,9},{9,8},{10,11... | collective-permute-start | bytes 147464 | tf_op jit(solution)/shard_map/ppermute | solution.py:519
  156.8 7.1 %collective-permute-start.13 = (bf16[3,64,128]{2,1,0:T(8,128)(2,1)S(1)}, bf16[3,64,128]{2,1,0:T(8,128)(2,1)S(1)}, u32[]{:S(2)}, u32[]{:S(2)}) collective-permute-start(bf16[3,64,128]{2,1,0:T(8,128)(2,1)S(1)} %get-tuple-element.85), channel_id=1, source_target_pairs={{1,2},{3,4},{5,6},{7,8},{9,10},{11,12},{13,14},{15,0},{2,1},{4,3},... | collective-permute-start | bytes 147464 | tf_op jit(solution)/shard_map/ppermute | solution.py:518
  164.0 4.2 %collective-permute-start.14 = (bf16[3,64,128]{2,1,0:T(8,128)(2,1)S(1)}, bf16[3,64,128]{2,1,0:T(8,128)(2,1)S(1)}, u32[]{:S(2)}, u32[]{:S(2)}) collective-permute-start(bf16[3,64,128]{2,1,0:T(8,128)(2,1)S(1)} %get-tuple-element.86), channel_id=1, source_target_pairs={{0,16},{16,0},{32,48},{48,32},{64,80},{80,64},{96,112},{112,96},{1... | collective-permute-start | bytes 147464 | tf_op jit(solution)/shard_map/ppermute | solution.py:519
  164.6 6.2 %collective-permute-start.15 = (bf16[3,64,128]{2,1,0:T(8,128)(2,1)S(1)}, bf16[3,64,128]{2,1,0:T(8,128)(2,1)S(1)}, u32[]{:S(2)}, u32[]{:S(2)}) collective-permute-start(bf16[3,64,128]{2,1,0:T(8,128)(2,1)S(1)} %get-tuple-element.87), channel_id=1, source_target_pairs={{16,32},{48,64},{80,96},{112,0},{32,16},{64,48},{96,80},{0,112},{1... | collective-permute-start | bytes 147464 | tf_op jit(solution)/shard_map/ppermute | solution.py:518
  (1 other events, 41.4 us)
where the time goes:
time: 175 us
  blocking collectives  75.5 us (43%)
  starting transfers between devices  45.3 us (26%)
  waiting for transfers between devices  27 us (15%)
  Pallas kernels  23.1 us (13%)
    all_to_all x4, blocking collectives, exchange(): return lax.all_to_all(value, axes, 0, 0, tiled=True)  75.5 us
    ppermute x8, starting transfers between devices, swaps(): far = lax.ppermute(far, axes, odd + [(b, a) for a, b in odd])  26 us
    ppermute x8, waiting for transfers between devices, swaps(): far = lax.ppermute(far, axes, odd + [(b, a) for a, b in odd])  21.6 us
    pallas_call x19, Pallas kernels, local(): pl.pallas_call(kernel, out_shape=[jax.ShapeDtypeStruct(s, d) for s, d in...  20.6 us
    all_to_all x2, starting transfers between devices, exchange(): return lax.all_to_all(value, axes, 0, 0, tiled=True)  12.7 us
    ppermute x8, starting transfers between devices, swaps(): near = lax.ppermute(near, axes, [(k, k ^ 1) for k in range(length)])  6.28 us
    ppermute x8, waiting for transfers between devices, swaps(): near = lax.ppermute(near, axes, [(k, k ^ 1) for k in range(length)])  3.67 us
  transfers between devices with their start and end apart: 21, of which 10 were waited for; matrix products, arithmetic and copies ran while one was open for 1% of the time, Pallas kernels for 7%

commit v1 on v0

--- a/solution.py
+++ b/solution.py
@@ -399,8 +399,20 @@
     send_gradients(acc, own, y_near_out, y_far_out, x_faces)
 
 
+def planes_kernel(meta, ext, planes, gathered):
+    shifted_planes(meta, ext, gathered, planes)
+
+
 def taps_kernel(meta, ext, dz, mine, other, gathered, planes, taps):
     shifted_planes(meta, ext, gathered, planes)
+    tap_halves(meta, planes, dz, mine, other, taps)
+
+
+def planes_taps_kernel(meta, planes, dz, mine, other, taps):
+    tap_halves(meta, planes, dz, mine, other, taps)
+
+
+def tap_halves(meta, planes, dz, mine, other, taps):
     for k in range(TAPS):
         taps[k * C : (k + 1) * C, :] = lax.dot_general(
             patches(planes, k),
@@ -614,6 +626,7 @@
     chunks = (32, CHUNK, C)
     halves = [(chunks, F32), (chunks, BF16)]
     products = [gathered, gathered, ((TAPS * C, C), F32)]
+    (planes_one,) = local(planes_kernel, [gathered], [meta, ext_one], [gathered])
     mine, other = local(taps_kernel, halves, [meta, ext_two, dz_two], products)
     (second,) = local(second_sum_kernel, [(chunks, BF16)], [mine, swap(other)])
     part = exchange(part, GX_GY)
@@ -631,7 +644,9 @@
         far=(2,),
     )
     returned = two_hops(y_near, y_far, x_faces, True)
-    mine, other = local(taps_kernel, halves, [meta, ext_one, dz_one], products)
+    mine, other = local(
+        planes_taps_kernel, halves, [meta, planes_one, dz_one], products[2:]
+    )
     grad_in, norm_grads = local(
         last_kernel,
         [(rows, BF16), ((4, C), F32)],

time: 175 us -> 175 us (level)
    pallas_call x19 -> x20, Pallas kernels: 20.6 us -> 21.9 us  [local(): pl.pallas_call(kernel, out_shape=[jax.ShapeDtypeStruct(s, d) for s, d in...]
  transfers between devices with their start and end apart: 21 -> 21, of which waited for: 10 -> 10; matrix products, arithmetic and copies ran while one was open for 1% -> 1% of each run, Pallas kernels for 7% -> 8%
where the time goes in v1:
time: 175 us; the launch traced here: 174 us
  blocking collectives  75.6 us (43%)
  starting transfers between devices  45 us (26%)
  waiting for transfers between devices  25.5 us (15%)
  Pallas kernels  24.5 us (14%)
    all_to_all x4, blocking collectives, exchange(): return lax.all_to_all(value, axes, 0, 0, tiled=True)  75.6 us
    ppermute x8, starting transfers between devices, swaps(): far = lax.ppermute(far, axes, odd + [(b, a) for a, b in odd])  26 us
    pallas_call x20, Pallas kernels, local(): pl.pallas_call(kernel, out_shape=[jax.ShapeDtypeStruct(s, d) for s, d in...  21.9 us
    ppermute x8, waiting for transfers between devices, swaps(): far = lax.ppermute(far, axes, odd + [(b, a) for a, b in odd])  20.1 us
    all_to_all x2, starting transfers between devices, exchange(): return lax.all_to_all(value, axes, 0, 0, tiled=True)  12.7 us
    ppermute x8, starting transfers between devices, swaps(): near = lax.ppermute(near, axes, [(k, k ^ 1) for k in range(length)])  6.26 us
    ppermute x8, waiting for transfers between devices, swaps(): near = lax.ppermute(near, axes, [(k, k ^ 1) for k in range(length)])  3.67 us
  transfers between devices with their start and end apart: 21, of which 10 were waited for; matrix products, arithmetic and copies ran while one was open for 1% of the time, Pallas kernels for 8%

profile of v1, /device:TPU:0, one launch (start us, length us, event | category | flops | bytes accessed | tf_op | source)
XLA Modules:
  0.0 174.4 jit_solution(5598758570353177834)
XLA Ops:
  1.7 6.7 %collective-permute-start.1 = (bf16[3,64,128]{2,1,0:T(8,128)(2,1)S(1)}, bf16[3,64,128]{2,1,0:T(8,128)(2,1)S(1)}, u32[]{:S(2)}, u32[]{:S(2)}) collective-permute-start(bf16[3,64,128]{2,1,0:T(8,128)(2,1)S(1)} %get-tuple-element.54), channel_id=1, source_target_pairs={{1,2},{3,4},{5,6},{7,8},{9,10},{11,12},{13,14},{15,0},{2,1},{4,3},... | collective-permute-start | bytes 147464 | tf_op jit(solution)/shard_map/ppermute | solution.py:530
  8.4 1.8 %collective-permute-done.1.y_far = bf16[3,64,128]{2,1,0:T(8,128)(2,1)S(1)} collective-permute-done((bf16[3,64,128]{2,1,0:T(8,128)(2,1)S(1)}, bf16[3,64,128]{2,1,0:T(8,128)(2,1)S(1)}, u32[]{:S(2)}, u32[]{:S(2)}) %collective-permute-start.1) | collective-permute-done | bytes 49184 | tf_op jit(solution)/shard_map/ppermute | solution.py:530
  11.8 2.2 %collective-permute-start.3 = (bf16[3,64,128]{2,1,0:T(8,128)(2,1)S(1)}, bf16[3,64,128]{2,1,0:T(8,128)(2,1)S(1)}, u32[]{:S(2)}, u32[]{:S(2)}) collective-permute-start(bf16[3,64,128]{2,1,0:T(8,128)(2,1)S(1)} %get-tuple-element.56), channel_id=1, source_target_pairs={{16,32},{48,64},{80,96},{112,0},{32,16},{64,48},{96,80},{0,112},{1... | collective-permute-start | bytes 147464 | tf_op jit(solution)/shard_map/ppermute | solution.py:530
  18.1 2.3 %shard_map.150 = (f32[4,64,128]{2,1,0:T(8,128)S(1)}, bf16[13,64,128]{2,1,0:T(8,128)(2,1)S(1)}, f32[512,128]{1,0:T(8,128)}, f32[3,64,128]{2,1,0:T(8,128)S(1)}, f3...) custom-call(s32[126]{0:T(128)S(1)} %concatenate.6.meta, bf16[4,64,128]{2,1,0:T(8,128)(2,1)S(1)} %get-tuple-element.51.voxel_feats, ...), custom_call_target="tpu_custom_call" | custom-call | tf_op jit(solution)/shard_map/pallas_call | solution.py:493
  20.5 7.8 %all-to-all-start = ((f32[128,4,128]{2,1,0:T(4,128)}), f32[128,4,128]{2,1,0:T(4,128)S(1)}, u32[]{:S(2)}, u32[]{:S(2)}) async-start(f32[128,4,128]{2,1,0:T(4,128)} %bitcast.4), calls=%async_computation | async-start | bytes 524288 | tf_op jit(solution)/shard_map/all_to_all | solution.py:520
  28.4 5.4 %collective-permute-start.5 = (f32[3,64,128]{2,1,0:T(8,128)S(1)}, f32[3,64,128]{2,1,0:T(8,128)S(1)}, u32[]{:S(2)}, u32[]{:S(2)}) collective-permute-start(f32[3,64,128]{2,1,0:T(8,128)S(1)} %get-tuple-element.61), channel_id=1, source_target_pairs={{1,2},{3,4},{5,6},{7,8},{9,10},{11,12},{13,14},{15,0},{2,1},{4,3},... | collective-permute-start | bytes 294920 | tf_op jit(solution)/shard_map/ppermute | solution.py:530
  34.9 3.3 %collective-permute-done.5.y_far = f32[3,64,128]{2,1,0:T(8,128)S(1)} collective-permute-done((f32[3,64,128]{2,1,0:T(8,128)S(1)}, f32[3,64,128]{2,1,0:T(8,128)S(1)}, u32[]{:S(2)}, u32[]{:S(2)}) %collective-permute-start.5) | collective-permute-done | bytes 98336 | tf_op jit(solution)/shard_map/ppermute | solution.py:530
  39.9 2.2 %collective-permute-start.7 = (f32[3,64,128]{2,1,0:T(8,128)S(1)}, f32[3,64,128]{2,1,0:T(8,128)S(1)}, u32[]{:S(2)}, u32[]{:S(2)}) collective-permute-start(f32[3,64,128]{2,1,0:T(8,128)S(1)} %get-tuple-element.63), channel_id=1, source_target_pairs={{16,32},{48,64},{80,96},{112,0},{32,16},{64,48},{96,80},{0,112},{1... | collective-permute-start | bytes 294920 | tf_op jit(solution)/shard_map/ppermute | solution.py:530
  43.0 3.6 %collective-permute-done.7.x_far = f32[3,64,128]{2,1,0:T(8,128)S(1)} collective-permute-done((f32[3,64,128]{2,1,0:T(8,128)S(1)}, f32[3,64,128]{2,1,0:T(8,128)S(1)}, u32[]{:S(2)}, u32[]{:S(2)}) %collective-permute-start.7) | collective-permute-done | bytes 98336 | tf_op jit(solution)/shard_map/ppermute | solution.py:530
  46.6 1.8 %shard_map.153 = (f32[256,128]{1,0:T(8,128)S(1)}, bf16[13,64,128]{2,1,0:T(8,128)(2,1)S(1)}, f32[256,128]{1,0:T(8,128)S(1)}, f32[12,64,128]{2,1,0:T(8,128)S(1)}, f32[16,128]{1,0:T(8,128)S(1)}) custom-call(s32[126]{0:T(128)S(1)} %concatenate.6.meta, f32[512,128]{1,0:T(8,128)S(1)} %bitcast.18, f32[4,64,128]{2,1,0:T(8,128)S(1)} %get-tuple-element.58.z_one, ...), custom_call_target="tpu_custom_call" | custom-call | tf_op jit(solution)/shard_map/pallas_call | solution.py:493
  48.4 15.5 %all_to_all.54 = f32[128,2,128]{2,1,0:T(2,128)S(1)} all-to-all(f32[128,2,128]{2,1,0:T(2,128)S(1)} %bitcast.23), channel_id=1, replica_groups=mesh['gx_0'=2,'gx_1'=4,'gy_0'=4,'gy_1'=2,'gy_2'=2] {'gx_0','gx_1','gy_0'..., dimensions={0} | all-to-all | bytes 262144 | tf_op jit(solution)/shard_map/all_to_all | solution.py:520
  65.2 14.2 %all_to_all.55 = f32[128,2,128]{2,1,0:T(2,128)S(1)} all-to-all(f32[128,2,128]{2,1,0:T(2,128)S(1)} %bitcast.24), channel_id=1, replica_groups=mesh['gx_0'=2,'gx_1'=4,'gy_0'=4,'gy_1'=2,'gy_2'=2] {'gx_0','gx_1','gy_0'..., dimensions={0} | all-to-all | bytes 262144 | tf_op jit(solution)/shard_map/all_to_all | solution.py:520
  79.3 2.9 %shard_map.155 = (bf16[256,128]{1,0:T(8,128)(2,1)S(1)}, f32[256,128]{1,0:T(8,128)S(1)}, bf16[3,64,128]{2,1,0:T(8,128)(2,1)S(1)}, bf16[3,64,128]{2,1,0:T(8,128)(2...) custom-call(s32[126]{0:T(128)S(1)} %concatenate.6.meta, ...), custom_call_target="tpu_custom_call" | custom-call | tf_op jit(solution)/shard_map/pallas_call | solution.py:493
  82.2 4.9 %all-to-all-start.3 = ((f32[128,2,128]{2,1,0:T(2,128)}), f32[128,2,128]{2,1,0:T(2,128)S(1)}, u32[]{:S(2)}, u32[]{:S(2)}) async-start(f32[128,2,128]{2,1,0:T(2,128)} %bitcast.14), calls=%async_computation.3 | async-start | bytes 262144 | tf_op jit(solution)/shard_map/all_to_all | solution.py:520
  87.2 5.4 %collective-permute-start.9 = (bf16[3,64,128]{2,1,0:T(8,128)(2,1)S(1)}, bf16[3,64,128]{2,1,0:T(8,128)(2,1)S(1)}, u32[]{:S(2)}, u32[]{:S(2)}) collective-permute-start(bf16[3,64,128]{2,1,0:T(8,128)(2,1)S(1)} %get-tuple-element.77), channel_id=1, source_target_pairs={{1,2},{3,4},{5,6},{7,8},{9,10},{11,12},{13,14},{15,0},{2,1},{4,3},... | collective-permute-start | bytes 147464 | tf_op jit(solution)/shard_map/ppermute | solution.py:530
  92.6 2.2 %collective-permute-done.9.y_far = bf16[3,64,128]{2,1,0:T(8,128)(2,1)S(1)} collective-permute-done((bf16[3,64,128]{2,1,0:T(8,128)(2,1)S(1)}, bf16[3,64,128]{2,1,0:T(8,128)(2,1)S(1)}, u32[]{:S(2)}, u32[]{:S(2)}) %collective-permute-start.9) | collective-permute-done | bytes 49184 | tf_op jit(solution)/shard_map/ppermute | solution.py:530
  96.4 2.1 %collective-permute-start.11 = (bf16[3,64,128]{2,1,0:T(8,128)(2,1)S(1)}, bf16[3,64,128]{2,1,0:T(8,128)(2,1)S(1)}, u32[]{:S(2)}, u32[]{:S(2)}) collective-permute-start(bf16[3,64,128]{2,1,0:T(8,128)(2,1)S(1)} %get-tuple-element.79), channel_id=1, source_target_pairs={{16,32},{48,64},{80,96},{112,0},{32,16},{64,48},{96,80},{0,112},{1... | collective-permute-start | bytes 147464 | tf_op jit(solution)/shard_map/ppermute | solution.py:530
  99.5 2.4 %shard_map.163 = (f32[32,56,128]{2,1,0:T(8,128)S(1)}, bf16[32,56,128]{2,1,0:T(8,128)(2,1)}) custom-call(s32[126]{0:T(128)S(1)} %concatenate.6.meta, bf16[13,64,128]{2,1,0:T(8,128)(2,1)S(1)} %get-tuple-element.93.ext, bf16[256,128]{1,0:T(8,128)(2,1)S(1)} %get-tuple-element.94.dz), custom_call_target="tpu_custom_call" | custom-call | tf_op jit(solution)/shard_map/pallas_call | solution.py:493
  106.5 25.0 %all_to_all.56.pieces = bf16[64,56,128]{2,1,0:T(8,128)(2,1)S(1)} all-to-all(bf16[64,56,128]{2,1,0:T(8,128)(2,1)S(1)} %shard_map.165), channel_id=1, replica_groups=mesh['gx_0'=2,'gx_1'=4,'gy_0'=4,'gy_1'=2,'gy_2'=2] {'gx_0','gx_1','gy_0'..., dimensions={0} | all-to-all | bytes 1835008 | tf_op jit(solution)/shard_map/all_to_all | solution.py:520
  131.7 20.9 %all_to_all.57.half = bf16[64,56,128]{2,1,0:T(8,128)(2,1)S(1)} all-to-all(bf16[64,56,128]{2,1,0:T(8,128)(2,1)S(1)} %shard_map.166), channel_id=1, replica_groups=mesh['gx_0'=2,'gx_1'=4,'gy_0'=4,'gy_1'=2,'gy_2'=2] {'gx_0','gx_1','gy_0'..., dimensions={0} | all-to-all | bytes 1835008 | tf_op jit(solution)/shard_map/all_to_all | solution.py:520
  152.6 3.2 %shard_map.158 = (f32[256,128]{1,0:T(8,128)S(1)}, bf16[3,64,128]{2,1,0:T(8,128)(2,1)S(1)}, bf16[3,64,128]{2,1,0:T(8,128)(2,1)S(1)}, bf16[2,64,128]{2,1,0:T(8,128)(2,1)S(1)}) custom-call(s32[126]{0:T(128)S(1)} %concatenate.6.meta, bf16[256,128]{1,0:T(8,128)(2,1)S(1)} %get-tuple-element.81.dz, bf16[3456,128]{1,0:T(8,128)(2,1)} %bitcast.28), custom_call_target="tpu_custom_call" | custom-call | tf_op jit(solution)/shard_map/pallas_call | solution.py:493
  157.6 5.9 %collective-permute-done.13.y_far = bf16[3,64,128]{2,1,0:T(8,128)(2,1)S(1)} collective-permute-done((bf16[3,64,128]{2,1,0:T(8,128)(2,1)S(1)}, bf16[3,64,128]{2,1,0:T(8,128)(2,1)S(1)}, u32[]{:S(2)}, u32[]{:S(2)}) %collective-permute-start.13) | collective-permute-done | bytes 49184 | tf_op jit(solution)/shard_map/ppermute | solution.py:530
  165.0 2.7 %collective-permute-done.14.x_near = bf16[3,64,128]{2,1,0:T(8,128)(2,1)S(1)} collective-permute-done((bf16[3,64,128]{2,1,0:T(8,128)(2,1)S(1)}, bf16[3,64,128]{2,1,0:T(8,128)(2,1)S(1)}, u32[]{:S(2)}, u32[]{:S(2)}) %collective-permute-start.14) | collective-permute-done | bytes 49184 | tf_op jit(solution)/shard_map/ppermute | solution.py:531
  167.7 2.7 %collective-permute-done.15.x_far = bf16[3,64,128]{2,1,0:T(8,128)(2,1)S(1)} collective-permute-done((bf16[3,64,128]{2,1,0:T(8,128)(2,1)S(1)}, bf16[3,64,128]{2,1,0:T(8,128)(2,1)S(1)}, u32[]{:S(2)}, u32[]{:S(2)}) %collective-permute-start.15) | collective-permute-done | bytes 49184 | tf_op jit(solution)/shard_map/ppermute | solution.py:530
  (56 shorter events, 25.8 us)
Async XLA Ops:
  0.6 41.4 %copy-start.2 = (f32[2,128]{1,0:T(2,128)S(1)}, f32[2,128]{1,0:T(2,128)}, u32[]{:S(2)}) copy-start(f32[2,128]{1,0:T(2,128)} %param.16) | copy-start | bytes 3076
  1.6 6.8 %collective-permute-start = (bf16[3,64,128]{2,1,0:T(8,128)(2,1)S(1)}, bf16[3,64,128]{2,1,0:T(8,128)(2,1)S(1)}, u32[]{:S(2)}, u32[]{:S(2)}) collective-permute-start(bf16[3,64,128]{2,1,0:T(8,128)(2,1)S(1)} %get-tuple-element.53), channel_id=1, source_target_pairs={{0,1},{1,0},{2,3},{3,2},{4,5},{5,4},{6,7},{7,6},{8,9},{9,8},{10,11... | collective-permute-start | bytes 147464 | tf_op jit(solution)/shard_map/ppermute | solution.py:531
  1.7 8.5 %collective-permute-start.1 = (bf16[3,64,128]{2,1,0:T(8,128)(2,1)S(1)}, bf16[3,64,128]{2,1,0:T(8,128)(2,1)S(1)}, u32[]{:S(2)}, u32[]{:S(2)}) collective-permute-start(bf16[3,64,128]{2,1,0:T(8,128)(2,1)S(1)} %get-tuple-element.54), channel_id=1, source_target_pairs={{1,2},{3,4},{5,6},{7,8},{9,10},{11,12},{13,14},{15,0},{2,1},{4,3},... | collective-permute-start | bytes 147464 | tf_op jit(solution)/shard_map/ppermute | solution.py:530
  10.2 7.9 %collective-permute-start.2 = (bf16[3,64,128]{2,1,0:T(8,128)(2,1)S(1)}, bf16[3,64,128]{2,1,0:T(8,128)(2,1)S(1)}, u32[]{:S(2)}, u32[]{:S(2)}) collective-permute-start(bf16[3,64,128]{2,1,0:T(8,128)(2,1)S(1)} %get-tuple-element.55), channel_id=1, source_target_pairs={{0,16},{16,0},{32,48},{48,32},{64,80},{80,64},{96,112},{112,96},{1... | collective-permute-start | bytes 147464 | tf_op jit(solution)/shard_map/ppermute | solution.py:531
  11.8 6.3 %collective-permute-start.3 = (bf16[3,64,128]{2,1,0:T(8,128)(2,1)S(1)}, bf16[3,64,128]{2,1,0:T(8,128)(2,1)S(1)}, u32[]{:S(2)}, u32[]{:S(2)}) collective-permute-start(bf16[3,64,128]{2,1,0:T(8,128)(2,1)S(1)} %get-tuple-element.56), channel_id=1, source_target_pairs={{16,32},{48,64},{80,96},{112,0},{32,16},{64,48},{96,80},{0,112},{1... | collective-permute-start | bytes 147464 | tf_op jit(solution)/shard_map/ppermute | solution.py:530
  16.1 47.7 %copy-start = (bf16[4,64,128]{2,1,0:T(8,128)(2,1)S(1)}, bf16[4,64,128]{2,1,0:T(8,128)(2,1)}, u32[]{:S(2)}) copy-start(bf16[4,64,128]{2,1,0:T(8,128)(2,1)} %field.1) | copy-start | bytes 196612
  16.1 47.7 %copy-start.1 = (bf16[4,64,128]{2,1,0:T(8,128)(2,1)S(1)}, bf16[4,64,128]{2,1,0:T(8,128)(2,1)}, u32[]{:S(2)}) copy-start(bf16[4,64,128]{2,1,0:T(8,128)(2,1)} %param.17) | copy-start | bytes 196612
  20.5 26.1 %all-to-all-start = ((f32[128,4,128]{2,1,0:T(4,128)}), f32[128,4,128]{2,1,0:T(4,128)S(1)}, u32[]{:S(2)}, u32[]{:S(2)}) async-start(f32[128,4,128]{2,1,0:T(4,128)} %bitcast.4), calls=%async_computation | async-start | bytes 524288 | tf_op jit(solution)/shard_map/all_to_all | solution.py:520
  28.3 6.6 %collective-permute-start.4 = (f32[3,64,128]{2,1,0:T(8,128)S(1)}, f32[3,64,128]{2,1,0:T(8,128)S(1)}, u32[]{:S(2)}, u32[]{:S(2)}) collective-permute-start(f32[3,64,128]{2,1,0:T(8,128)S(1)} %get-tuple-element.60), channel_id=1, source_target_pairs={{0,1},{1,0},{2,3},{3,2},{4,5},{5,4},{6,7},{7,6},{8,9},{9,8},{10,11... | collective-permute-start | bytes 294920 | tf_op jit(solution)/shard_map/ppermute | solution.py:531
  28.4 9.9 %collective-permute-start.5 = (f32[3,64,128]{2,1,0:T(8,128)S(1)}, f32[3,64,128]{2,1,0:T(8,128)S(1)}, u32[]{:S(2)}, u32[]{:S(2)}) collective-permute-start(f32[3,64,128]{2,1,0:T(8,128)S(1)} %get-tuple-element.61), channel_id=1, source_target_pairs={{1,2},{3,4},{5,6},{7,8},{9,10},{11,12},{13,14},{15,0},{2,1},{4,3},... | collective-permute-start | bytes 294920 | tf_op jit(solution)/shard_map/ppermute | solution.py:530
  38.3 4.7 %collective-permute-start.6 = (f32[3,64,128]{2,1,0:T(8,128)S(1)}, f32[3,64,128]{2,1,0:T(8,128)S(1)}, u32[]{:S(2)}, u32[]{:S(2)}) collective-permute-start(f32[3,64,128]{2,1,0:T(8,128)S(1)} %get-tuple-element.62), channel_id=1, source_target_pairs={{0,16},{16,0},{32,48},{48,32},{64,80},{80,64},{96,112},{112,96},{1... | collective-permute-start | bytes 294920 | tf_op jit(solution)/shard_map/ppermute | solution.py:531
  39.9 6.7 %collective-permute-start.7 = (f32[3,64,128]{2,1,0:T(8,128)S(1)}, f32[3,64,128]{2,1,0:T(8,128)S(1)}, u32[]{:S(2)}, u32[]{:S(2)}) collective-permute-start(f32[3,64,128]{2,1,0:T(8,128)S(1)} %get-tuple-element.63), channel_id=1, source_target_pairs={{16,32},{48,64},{80,96},{112,0},{32,16},{64,48},{96,80},{0,112},{1... | collective-permute-start | bytes 294920 | tf_op jit(solution)/shard_map/ppermute | solution.py:530
  82.2 20.3 %all-to-all-start.3 = ((f32[128,2,128]{2,1,0:T(2,128)}), f32[128,2,128]{2,1,0:T(2,128)S(1)}, u32[]{:S(2)}, u32[]{:S(2)}) async-start(f32[128,2,128]{2,1,0:T(2,128)} %bitcast.14), calls=%async_computation.3 | async-start | bytes 262144 | tf_op jit(solution)/shard_map/all_to_all | solution.py:520
  87.1 5.5 %collective-permute-start.8 = (bf16[3,64,128]{2,1,0:T(8,128)(2,1)S(1)}, bf16[3,64,128]{2,1,0:T(8,128)(2,1)S(1)}, u32[]{:S(2)}, u32[]{:S(2)}) collective-permute-start(bf16[3,64,128]{2,1,0:T(8,128)(2,1)S(1)} %get-tuple-element.76), channel_id=1, source_target_pairs={{0,1},{1,0},{2,3},{3,2},{4,5},{5,4},{6,7},{7,6},{8,9},{9,8},{10,11... | collective-permute-start | bytes 147464 | tf_op jit(solution)/shard_map/ppermute | solution.py:531
  87.2 7.6 %collective-permute-start.9 = (bf16[3,64,128]{2,1,0:T(8,128)(2,1)S(1)}, bf16[3,64,128]{2,1,0:T(8,128)(2,1)S(1)}, u32[]{:S(2)}, u32[]{:S(2)}) collective-permute-start(bf16[3,64,128]{2,1,0:T(8,128)(2,1)S(1)} %get-tuple-element.77), channel_id=1, source_target_pairs={{1,2},{3,4},{5,6},{7,8},{9,10},{11,12},{13,14},{15,0},{2,1},{4,3},... | collective-permute-start | bytes 147464 | tf_op jit(solution)/shard_map/ppermute | solution.py:530
  94.8 7.1 %collective-permute-start.10 = (bf16[3,64,128]{2,1,0:T(8,128)(2,1)S(1)}, bf16[3,64,128]{2,1,0:T(8,128)(2,1)S(1)}, u32[]{:S(2)}, u32[]{:S(2)}) collective-permute-start(bf16[3,64,128]{2,1,0:T(8,128)(2,1)S(1)} %get-tuple-element.78), channel_id=1, source_target_pairs={{0,16},{16,0},{32,48},{48,32},{64,80},{80,64},{96,112},{112,96},{1... | collective-permute-start | bytes 147464 | tf_op jit(solution)/shard_map/ppermute | solution.py:531
  96.4 6.2 %collective-permute-start.11 = (bf16[3,64,128]{2,1,0:T(8,128)(2,1)S(1)}, bf16[3,64,128]{2,1,0:T(8,128)(2,1)S(1)}, u32[]{:S(2)}, u32[]{:S(2)}) collective-permute-start(bf16[3,64,128]{2,1,0:T(8,128)(2,1)S(1)} %get-tuple-element.79), channel_id=1, source_target_pairs={{16,32},{48,64},{80,96},{112,0},{32,16},{64,48},{96,80},{0,112},{1... | collective-permute-start | bytes 147464 | tf_op jit(solution)/shard_map/ppermute | solution.py:530
  101.9 2.7 %collective-permute-start.17 = (bf16[32,56,128]{2,1,0:T(8,128)(2,1)}, bf16[32,56,128]{2,1,0:T(8,128)(2,1)S(1)}, u32[]{:S(2)}, u32[]{:S(2)}) collective-permute-start(bf16[32,56,128]{2,1,0:T(8,128)(2,1)} %get-tuple-element.96), channel_id=1, source_target_pairs={{0,1},{1,0},{2,3},{3,2},{4,5},{5,4},{6,7},{7,6},{8,9},{9,8},{10,11... | collective-permute-start | bytes 1376264 | tf_op jit(solution)/shard_map/ppermute | solution.py:524
  104.5 1.9 %collective-permute-start.16 = (bf16[32,56,128]{2,1,0:T(8,128)(2,1)S(1)}, bf16[32,56,128]{2,1,0:T(8,128)(2,1)S(1)}, u32[]{:S(2)}, u32[]{:S(2)}) collective-permute-start(bf16[32,56,128]{2,1,0:T(8,128)(2,1)S(1)} %get-tuple-element.92), channel_id=1, source_target_pairs={{0,1},{1,0},{2,3},{3,2},{4,5},{5,4},{6,7},{7,6},{8,9},{9,8},{10,11... | collective-permute-start | bytes 1376264 | tf_op jit(solution)/shard_map/ppermute | solution.py:524
  152.6 20.3 %collective-permute-start.18 = (bf16[64,56,128]{2,1,0:T(8,128)(2,1)S(1)}, bf16[64,56,128]{2,1,0:T(8,128)(2,1)S(1)}, u32[]{:S(2)}, u32[]{:S(2)}) collective-permute-start(bf16[64,56,128]{2,1,0:T(8,128)(2,1)S(1)} %all_to_all.57.half), channel_id=1, source_target_pairs={{0,1},{1,0},{2,3},{3,2},{4,5},{5,4},{6,7},{7,6},{8,9},{9,8},{10,11... | collective-permute-start | bytes 2752520 | tf_op jit(solution)/shard_map/ppermute | solution.py:524
  155.9 1.8 %collective-permute-start.12 = (bf16[3,64,128]{2,1,0:T(8,128)(2,1)S(1)}, bf16[3,64,128]{2,1,0:T(8,128)(2,1)S(1)}, u32[]{:S(2)}, u32[]{:S(2)}) collective-permute-start(bf16[3,64,128]{2,1,0:T(8,128)(2,1)S(1)} %get-tuple-element.84), channel_id=1, source_target_pairs={{0,1},{1,0},{2,3},{3,2},{4,5},{5,4},{6,7},{7,6},{8,9},{9,8},{10,11... | collective-permute-start | bytes 147464 | tf_op jit(solution)/shard_map/ppermute | solution.py:531
  156.4 7.1 %collective-permute-start.13 = (bf16[3,64,128]{2,1,0:T(8,128)(2,1)S(1)}, bf16[3,64,128]{2,1,0:T(8,128)(2,1)S(1)}, u32[]{:S(2)}, u32[]{:S(2)}) collective-permute-start(bf16[3,64,128]{2,1,0:T(8,128)(2,1)S(1)} %get-tuple-element.85), channel_id=1, source_target_pairs={{1,2},{3,4},{5,6},{7,8},{9,10},{11,12},{13,14},{15,0},{2,1},{4,3},... | collective-permute-start | bytes 147464 | tf_op jit(solution)/shard_map/ppermute | solution.py:530
  163.5 4.2 %collective-permute-start.14 = (bf16[3,64,128]{2,1,0:T(8,128)(2,1)S(1)}, bf16[3,64,128]{2,1,0:T(8,128)(2,1)S(1)}, u32[]{:S(2)}, u32[]{:S(2)}) collective-permute-start(bf16[3,64,128]{2,1,0:T(8,128)(2,1)S(1)} %get-tuple-element.86), channel_id=1, source_target_pairs={{0,16},{16,0},{32,48},{48,32},{64,80},{80,64},{96,112},{112,96},{1... | collective-permute-start | bytes 147464 | tf_op jit(solution)/shard_map/ppermute | solution.py:531
  164.2 6.2 %collective-permute-start.15 = (bf16[3,64,128]{2,1,0:T(8,128)(2,1)S(1)}, bf16[3,64,128]{2,1,0:T(8,128)(2,1)S(1)}, u32[]{:S(2)}, u32[]{:S(2)}) collective-permute-start(bf16[3,64,128]{2,1,0:T(8,128)(2,1)S(1)} %get-tuple-element.87), channel_id=1, source_target_pairs={{16,32},{48,64},{80,96},{112,0},{32,16},{64,48},{96,80},{0,112},{1... | collective-permute-start | bytes 147464 | tf_op jit(solution)/shard_map/ppermute | solution.py:530
  (1 other events, 41.4 us)
